TPU v7x, 512 devices: a whole 4x8x8 slice. The times are simulated.
512 devices in a mesh: gx: 32 (over y, x), gy: 16 (over z, core).
Axes of the slice: x: 4, y: 8, z: 8, core: 2. Of those that a mesh axis runs over, the one named last changes fastest.
Arguments:
- diag_blocks: float32 [9, 2048, 2048], P(None, 'gx', 'gy'), may hold values from 0 to 36, as said below
- edge_blocks: float32 [4, 9, 2048, 2048], P(None, None, 'gx', 'gy'), may hold values from -0.3 to 0.3
- edge_mask: int32 [4, 2048, 2048], P(None, 'gx', 'gy'), may hold values 0 or 1
- src_values: float32 [3, 524288], P(None, ('gx', 'gy')), may hold values from -48 to 48
- src_owner: int32 [524288, 1], P(('gx', 'gy')), may hold values from 0 to 31; in each aligned block of 1024 rows (0 to 1023, 1024 to 2047, ...) at most 64 rows name the same one
- src_node: int32 [524288], P(('gx', 'gy')), may hold values from 0 to 8191
- src_count: int32 [512], P(('gx', 'gy')), may hold values from 256 to 1024, as said below
- surf_node: int32 [1048576], P(('gx', 'gy')), may hold values from 0 to 8191
- surf_param: float32 [3, 1048576], P(None, ('gx', 'gy')), may hold values from 0 to 1
- tile_box: int32 [8192], P(('gx', 'gy')), may hold values from 0 to 511
Outputs:
- adjoint_field: float32 [3, 2048, 2048], P(None, 'gx', 'gy')
- box_gradient: float32 [512, 192], P(('gx', 'gy'))
Inputs may be any that keep to these rules, and one draw needn't show every extreme that they name: `src_owner`: each device's rows name every gx index at most 64 times. `src_count`: some device has all 1024 rows live. `diag_blocks`: entries 0, 4 and 8 lie between 6 and 36; the other entries between 0 and 1.
All inputs are finite; a program needn't handle non-finite values. No bound on the sum of `edge_mask` on one device may be relied on, other than what follows from the above.
Results may differ from a plain program's by a relative error of at most 0.0015.
Values sent between devices are 32-bit elements; how exact they have to be, the bound alone decides.
A program may use at most 64 MiB of HBM per device.

v0:
```python
import jax
import jax.numpy as jnp
from jax import lax
from jax.sharding import PartitionSpec as P

ITERS = 2


def passed_along(block, axis, distance):
    devices = range(lax.axis_size(axis))
    route = [(i - distance, i) for i in devices if i - distance in devices]
    return lax.ppermute(block, axis, route)


def block_product(blocks, field):
    return jnp.stack(
        [
            blocks[row] * field[0] + blocks[3 + row] * field[1] + blocks[6 + row] * field[2]
            for row in range(3)
        ]
    )


def apply_transposed_operator(field, diag_blocks, masked):
    result = block_product(diag_blocks, field)
    toward_upx = block_product(masked[0], field)
    toward_lowx = block_product(masked[1], field)
    toward_upy = block_product(masked[2], field)
    toward_lowy = block_product(masked[3], field)
    from_below_x = passed_along(toward_upx[:, -1:, :], "gx", 1)
    upper_x = jnp.concatenate([from_below_x, toward_upx[:, :-1, :]], axis=1)
    from_above_x = passed_along(toward_lowx[:, :1, :], "gx", -1)
    lower_x = jnp.concatenate([toward_lowx[:, 1:, :], from_above_x], axis=1)
    from_below_y = passed_along(toward_upy[:, :, -1:], "gy", 1)
    upper_y = jnp.concatenate([from_below_y, toward_upy[:, :, :-1]], axis=2)
    from_above_y = passed_along(toward_lowy[:, :, :1], "gy", -1)
    lower_y = jnp.concatenate([toward_lowy[:, :, 1:], from_above_y], axis=2)
    return result + upper_x + lower_x + upper_y + lower_y


def bernstein(coord):
    other = 1.0 - coord
    return jnp.stack(
        [
            other * other * other,
            3.0 * coord * other * other,
            3.0 * coord * coord * other,
            coord * coord * coord,
        ]
    )


def tile_weights(params):
    first = bernstein(params[0])
    second = bernstein(params[1])
    third = bernstein(params[2])
    table = first[:, None, None, :] * second[None, :, None, :] * third[None, None, :, :]
    return table.reshape(64, -1)


def residual_sum(residual, precond):
    return lax.psum(jnp.sum(residual * precond), ("gx", "gy"))


def per_device(
    diag_blocks,
    edge_blocks,
    edge_mask,
    src_values,
    src_owner,
    src_node,
    src_count,
    surf_node,
    surf_param,
    tile_box,
):
    masked = edge_blocks * edge_mask.astype(jnp.float32)[:, None]
    cells_x = diag_blocks.shape[1]
    cells_y = diag_blocks.shape[2]
    rows = src_node.shape[0]
    flat_load = jnp.zeros((3, cells_x * cells_y), jnp.float32)
    all_values, every_owner_index, all_node, all_count = (
        lax.all_gather(src_values, "gx", axis=1, tiled=True),
        lax.all_gather(src_owner, "gx", axis=0, tiled=True),
        lax.all_gather(src_node, "gx", axis=0, tiled=True),
        lax.all_gather(src_count, "gx", axis=0, tiled=True),
    )
    position = jnp.arange(all_node.shape[0], dtype=jnp.int32)
    live = position % rows < jnp.repeat(all_count, rows)
    keeper = live & (every_owner_index[:, 0] == lax.axis_index("gx"))
    flat_load = flat_load.at[:, all_node].add(all_values * keeper.astype(jnp.float32))
    load = flat_load.reshape(3, cells_x, cells_y)
    scale = jnp.stack([diag_blocks[0], diag_blocks[4], diag_blocks[8]])
    solution = jnp.zeros_like(load)
    residual = load
    precond = residual / scale
    search = precond
    norm_now = residual_sum(residual, precond)
    for sweep in range(ITERS):
        image = apply_transposed_operator(search, diag_blocks, masked)
        step_size = norm_now / lax.psum(jnp.sum(search * image), ("gx", "gy"))
        solution = solution + step_size * search
        residual = residual - step_size * image
        if sweep + 1 < ITERS:
            precond = residual / scale
            norm_next = residual_sum(residual, precond)
            search = precond + norm_next / norm_now * search
            norm_now = norm_next
    design_sensitivity = solution.reshape(3, -1)[:, surf_node]
    tile_weight_values = tile_weights(surf_param)
    surface_tiles = tile_box.shape[0]
    series_terms = jnp.einsum(
        "bqe,iqe->qib",
        tile_weight_values.reshape(64, surface_tiles, -1),
        design_sensitivity.reshape(3, surface_tiles, -1),
        precision=lax.Precision.HIGHEST,
    ).reshape(surface_tiles, 192)
    box_count = lax.axis_size("gx") * lax.axis_size("gy")
    onehot = (jnp.arange(box_count, dtype=jnp.int32)[:, None] == tile_box[None, :]).astype(
        jnp.float32
    )
    partial_boxes = jnp.dot(onehot, series_terms, precision=lax.Precision.HIGHEST)
    totals = lax.psum(partial_boxes, ("gx", "gy"))
    gradient = lax.dynamic_slice_in_dim(totals, lax.axis_index(("gx", "gy")), 1, 0)
    return (solution, gradient)


def solution(mesh):
    return jax.shard_map(
        per_device,
        mesh=mesh,
        in_specs=(
            P(None, "gx", "gy"),
            P(None, None, "gx", "gy"),
            P(None, "gx", "gy"),
            P(None, ("gx", "gy")),
            P(("gx", "gy"), None),
            P(("gx", "gy")),
            P(("gx", "gy")),
            P(("gx", "gy")),
            P(None, ("gx", "gy")),
            P(("gx", "gy")),
        ),
        out_specs=(P(None, "gx", "gy"), P(("gx", "gy"), None)),
        check_vma=False,
    )
```

profile of v0, /device:TPU:24, one launch (start us, length us, event | category | flops | bytes accessed | tf_op | source)
XLA Modules:
  0.0 972.0 jit_solution(12247643676694862051)
XLA Ops:
  7.2 39.1 %all_gather.15 = s32[32768,1]{0,1:T(1,128)S(1)} all-gather(s32[1024,1]{0,1:T(1,128)} %param.14), channel_id=1, replica_groups=mesh['gx'=32,'gy'=16] {'gx'}, dimensions={0}, use_global_device_ids=true | all-gather | bytes 135168 | tf_op jit(solution)/shard_map/all_gather | solution.py:84
  46.9 1.3 dynamic-slice
  48.2 0.8 dynamic-update-slice
  49.0 17.6 %all-reduce = s32[32]{0:T(128)S(1)} all-reduce(s32[32]{0:T(128)S(1)} %dynamic-update-slice), channel_id=1, replica_groups=mesh['gx'=32,'gy'=16] {'gx'}, use_global_device_ids=true, to_apply=%add | all-reduce | flops 32 | bytes 256
  66.7 48.2 %all_gather.13 = f32[3,32768]{1,0:T(4,128)S(1)} all-gather(f32[3,1024]{1,0:T(4,128)} %param.13), channel_id=1, replica_groups=mesh['gx'=32,'gy'=16] {'gx'}, dimensions={1}, use_global_device_ids=true | all-gather | bytes 405504 | tf_op jit(solution)/shard_map/all_gather | solution.py:83
  115.5 8.6 copy.63
  124.1 36.8 %all_gather.12 = s32[32768]{0:T(1024)S(1)} all-gather(s32[1024]{0:T(1024)S(1)} %copy-done.6), channel_id=1, replica_groups=mesh['gx'=32,'gy'=16] {'gx'}, dimensions={0}, use_global_device_ids=true | all-gather | bytes 135168 | tf_op jit(solution)/shard_map/all_gather | solution.py:85
  160.9 176.4 %scatter_custom_fusion = f32[3,8192]{0,1:T(8,128)} fusion(s32[32768]{0:T(1024)S(1)} %compare_select_fusion, f32[32768,3]{1,0:T(8,128)} %copy.63, f32[]{:T(128)} %constant.12.clone.1), kind=kCustom, calls=%fused_computation.2 | custom fusion | flops 98304 | bytes 98816 | tf_op jit(solution)/shard_map/scatter-add | solution.py:91
  337.3 3.0 copy.66
  341.1 2.5 collective-permute-start
  344.2 5.5 collective-permute-start.1
  350.5 1.3 collective-permute-start.2
  351.8 1.3 collective-permute-start.3
  354.2 2.8 copy.65
  357.7 1.8 multiply_reduce_fusion.1
  359.6 105.4 %all-reduce.1 = (f32[]{:T(128)}, f32[]{:T(128)}) all-reduce(f32[]{:T(128)} %get-tuple-element.3, f32[]{:T(128)} %get-tuple-element.2), channel_id=1, replica_groups=mesh['gx'=32,'gy'=16] {'gx','gy'}, use_global_device_ids=true, to_apply=%region_2.3 | all-reduce | flops 2 | bytes 16 | tf_op jit(solution)/shard_map/psum | solution.py:62
  466.3 0.7 multiply_reduce_fusion
  467.0 96.2 %psum.37 = f32[]{:T(128)} all-reduce(f32[]{:T(128)} %get-tuple-element.6), channel_id=1, replica_groups=mesh['gx'=32,'gy'=16] {'gx','gy'}, use_global_device_ids=true, to_apply=%region_6.7 | all-reduce | flops 1 | bytes 8 | tf_op jit(solution)/shard_map/psum | solution.py:62
  564.5 0.9 fusion.21
  565.6 3.1 collective-permute-start.4
  568.8 4.9 collective-permute-start.5
  573.7 1.6 collective-permute-start.6
  575.5 1.3 collective-permute-start.7
  576.9 1.8 collective-permute-done.7
  578.8 0.9 fusion.7
  579.7 100.5 %psum.38 = f32[]{:T(128)} all-reduce(f32[]{:T(128)} %fusion.7), channel_id=1, replica_groups=mesh['gx'=32,'gy'=16] {'gx','gy'}, use_global_device_ids=true, to_apply=%region_8.9 | all-reduce | flops 1 | bytes 8 | tf_op jit(solution)/shard_map/psum | solution.py:101
  681.6 2.6 copy.69
  684.2 7.7 gather_fusion
  691.9 1.8 fusion.2
  693.8 1.2 fusion.4
  695.7 268.2 %all-reduce.4.cloned.1.call-done = f32[512,192]{1,0:T(8,128)} async-done(((f32[512,192]{1,0:T(8,128)}), f32[512,192]{1,0:T(8,128)}) %all-reduce.4.cloned.1.call-update) | async-done | bytes 393232 | tf_op jit(solution)/shard_map/psum | solution.py:123
  963.9 1.3 constant_dynamic-slice_fusion
  (80 shorter events, 6.0 us)
Async XLA Ops:
  7.2 956.7 %all-reduce.4.cloned.1.call-start = ((), (), s32[]{:S(2)}) async-start(), calls=%async_computation | async-start | bytes 1048576 | tf_op jit(solution)/shard_map/psum | solution.py:123
  115.5 8.6 copy-start.6
  337.3 3.0 copy-start
  337.3 3.0 copy-start.3
  337.3 3.0 copy-start.1
  341.1 16.6 %collective-permute-start = (f32[3,1,128]{2,1,0:T(1,128)}, f32[3,1,128]{2,1,0:T(1,128)S(1)}, u32[]{:S(2)}, u32[]{:S(2)}) collective-permute-start(f32[3,1,128]{2,1,0:T(1,128)} %pad_maximum_fusion.21), channel_id=1, source_target_pairs={{0,16},{16,32},{32,48},{48,64},{64,80},{80,96},{96,112},{112,128},... | collective-permute-start | bytes 4616 | tf_op jit(solution)/shard_map/ppermute | solution.py:12
  343.6 10.2 %copy-start.5 = (s32[2048]{0:T(1024)S(1)}, s32[2048]{0:T(1024)}, u32[]{:S(2)}) copy-start(s32[2048]{0:T(1024)} %param.17) | copy-start | bytes 24580
  343.6 10.1 %copy-start.4 = (f32[3,2048]{1,0:T(4,128)S(1)}, f32[3,2048]{1,0:T(4,128)}, u32[]{:S(2)}) copy-start(f32[3,2048]{1,0:T(4,128)} %param.18) | copy-start | bytes 73732
  344.2 13.5 %collective-permute-start.1 = (f32[3,1,128]{2,1,0:T(1,128)}, f32[3,1,128]{2,1,0:T(1,128)S(1)}, u32[]{:S(2)}, u32[]{:S(2)}) collective-permute-start(f32[3,1,128]{2,1,0:T(1,128)} %pad_maximum_fusion.20), channel_id=1, source_target_pairs={{16,0},{32,16},{48,32},{64,48},{80,64},{96,80},{112,96},{128,112},... | collective-permute-start | bytes 4616 | tf_op jit(solution)/shard_map/ppermute | solution.py:12
  350.5 6.9 collective-permute-start.2
  351.8 5.8 collective-permute-start.3
  357.4 207.1 %copy-start.2 = (f32[1,64,128]{2,1,0:T(8,128)S(1)}, f32[1,64,128]{2,1,0:T(8,128)}, u32[]{:S(2)}) copy-start(f32[1,64,128]{2,1,0:T(8,128)} %get-tuple-element.37) | copy-start | bytes 98308
  565.6 13.1 %collective-permute-start.4 = (f32[3,1,128]{2,1,0:T(1,128)S(1)}, f32[3,1,128]{2,1,0:T(1,128)S(1)}, u32[]{:S(2)}, u32[]{:S(2)}) collective-permute-start(f32[3,1,128]{2,1,0:T(1,128)S(1)} %pad_maximum_fusion.19), channel_id=1, source_target_pairs={{0,16},{16,32},{32,48},{48,64},{64,80},{80,96},{96,112},{112,128},... | collective-permute-start | bytes 4616 | tf_op jit(solution)/shard_map/ppermute | solution.py:12
  568.8 10.0 %collective-permute-start.5 = (f32[3,1,128]{2,1,0:T(1,128)S(1)}, f32[3,1,128]{2,1,0:T(1,128)S(1)}, u32[]{:S(2)}, u32[]{:S(2)}) collective-permute-start(f32[3,1,128]{2,1,0:T(1,128)S(1)} %pad_maximum_fusion.18), channel_id=1, source_target_pairs={{16,0},{32,16},{48,32},{64,48},{80,64},{96,80},{112,96},{128,112},... | collective-permute-start | bytes 4616 | tf_op jit(solution)/shard_map/ppermute | solution.py:12
  573.7 3.0 collective-permute-start.6
  575.5 3.2 collective-permute-start.7
  684.2 9.6 copy-start.7
Sparse Core Ops, SparseCore 0:
  695.1 268.6 all-reduce.3
where the time goes:
time: 973 us; the launch traced here: 972 us
  blocking collectives  444 us (46%)
  waiting for transfers between devices  270 us (28%)
  other arithmetic  185 us (19%)
  local copies, waits for them, and re-layouts  29.5 us (3%)
  starting transfers between devices  21.4 us (2%)
  between operations  19.3 us (2%)
    psum x1, waiting for transfers between devices, per_device(): totals = lax.psum(partial_boxes, ('gx', 'gy'))  268 us
    psum x2, blocking collectives, residual_sum(): return lax.psum(jnp.sum(residual * precond), ('gx', 'gy'))  202 us
    scatter-add x1, other arithmetic, per_device(): flat_load.at[:, all_node].add(all_values * keeper.astype(jnp.float32))  176 us
    psum x1, blocking collectives, per_device(): step_size = norm_now / lax.psum(jnp.sum(search * image), ('gx', 'gy'))  100 us
    all_gather x1, blocking collectives, per_device(): lax.all_gather(src_values, 'gx', axis=1, tiled=True)  48.2 us
    all_gather x1, blocking collectives, per_device(): lax.all_gather(src_owner, 'gx', axis=0, tiled=True)  39.1 us
    all_gather x1, blocking collectives, per_device(): lax.all_gather(src_node, 'gx', axis=0, tiled=True)  36.8 us
    ppermute x8, starting transfers between devices, passed_along(): return lax.ppermute(block, axis, route)  21.4 us
  transfers between devices with their start and end apart: 9, of which 3 were waited for; matrix products, arithmetic and copies ran while one was open for 1% of the time, Pallas kernels for 0%

commit v1 on v0

--- a/solution.py
+++ b/solution.py
@@ -120,7 +120,7 @@
         jnp.float32
     )
     partial_boxes = jnp.dot(onehot, series_terms, precision=lax.Precision.HIGHEST)
-    totals = lax.psum(partial_boxes, ("gx", "gy"))
+    totals = lax.psum(lax.psum(partial_boxes, "gx"), "gy")
     gradient = lax.dynamic_slice_in_dim(totals, lax.axis_index(("gx", "gy")), 1, 0)
     return (solution, gradient)
 

time: 973 us -> 974 us (level)
  the two profiles are of different devices: /device:TPU:24 before, /device:TPU:1 now
where the time goes in v1:
time: 974 us; the launch traced here: 973 us
  blocking collectives  411 us (42%)
  waiting for transfers between devices  276 us (28%)
  other arithmetic  182 us (19%)
  starting transfers between devices  52.3 us (5%)
  local copies, waits for them, and re-layouts  28.9 us (3%)
  between operations  19.3 us (2%)
    psum x2, waiting for transfers between devices, per_device(): totals = lax.psum(lax.psum(partial_boxes, 'gx'), 'gy')  272 us
    psum x2, blocking collectives, residual_sum(): return lax.psum(jnp.sum(residual * precond), ('gx', 'gy'))  201 us
    scatter-add x1, other arithmetic, per_device(): flat_load.at[:, all_node].add(all_values * keeper.astype(jnp.float32))  176 us
    psum x1, blocking collectives, per_device(): step_size = norm_now / lax.psum(jnp.sum(search * image), ('gx', 'gy'))  99.6 us
    ppermute x8, starting transfers between devices, passed_along(): return lax.ppermute(block, axis, route)  52.2 us
    all_gather x1, blocking collectives, per_device(): lax.all_gather(src_values, 'gx', axis=1, tiled=True)  36 us
    all_gather x1, blocking collectives, per_device(): lax.all_gather(src_owner, 'gx', axis=0, tiled=True)  32.4 us
    all_gather x1, blocking collectives, per_device(): lax.all_gather(src_node, 'gx', axis=0, tiled=True)  29.8 us
  transfers between devices with their start and end apart: 10, of which 4 were waited for; matrix products, arithmetic and copies ran while one was open for 0% of the time, Pallas kernels for 0%

profile of v1, /device:TPU:1, one launch (start us, length us, event | category | flops | bytes accessed | tf_op | source)
XLA Modules:
  0.0 973.2 jit_solution(2934652766072731491)
XLA Ops:
  7.2 32.4 %all_gather.15 = s32[32768,1]{0,1:T(1,128)S(1)} all-gather(s32[1024,1]{0,1:T(1,128)} %param.14), channel_id=1, replica_groups=mesh['gx'=32,'gy'=16] {'gx'}, dimensions={0}, use_global_device_ids=true | all-gather | bytes 135168 | tf_op jit(solution)/shard_map/all_gather | solution.py:84
  40.3 1.3 dynamic-slice
  41.5 0.8 dynamic-update-slice
  42.3 13.0 %all-reduce = s32[32]{0:T(128)S(1)} all-reduce(s32[32]{0:T(128)S(1)} %dynamic-update-slice), channel_id=1, replica_groups=mesh['gx'=32,'gy'=16] {'gx'}, use_global_device_ids=true, to_apply=%add | all-reduce | flops 32 | bytes 256
  55.4 36.0 %all_gather.13 = f32[3,32768]{1,0:T(4,128)S(1)} all-gather(f32[3,1024]{1,0:T(4,128)} %param.13), channel_id=1, replica_groups=mesh['gx'=32,'gy'=16] {'gx'}, dimensions={1}, use_global_device_ids=true | all-gather | bytes 405504 | tf_op jit(solution)/shard_map/all_gather | solution.py:83
  92.0 8.6 copy.63
  100.6 29.8 %all_gather.12 = s32[32768]{0:T(1024)S(1)} all-gather(s32[1024]{0:T(1024)S(1)} %copy-done.5), channel_id=1, replica_groups=mesh['gx'=32,'gy'=16] {'gx'}, dimensions={0}, use_global_device_ids=true | all-gather | bytes 135168 | tf_op jit(solution)/shard_map/all_gather | solution.py:85
  130.4 176.4 %scatter_custom_fusion = f32[3,8192]{0,1:T(8,128)} fusion(s32[32768]{0:T(1024)S(1)} %compare_select_fusion, f32[32768,3]{1,0:T(8,128)} %copy.63, f32[]{:T(128)} %constant.12.clone.1), kind=kCustom, calls=%fused_computation.2 | custom fusion | flops 98304 | bytes 98816 | tf_op jit(solution)/shard_map/scatter-add | solution.py:91
  306.8 3.0 copy.66
  310.1 1.9 collective-permute-start
  312.1 1.3 collective-permute-start.1
  313.6 37.0 %collective-permute-start.2 = (f32[3,64,1]{2,1,0:T(8,128)S(1)}, f32[3,64,1]{2,1,0:T(8,128)S(1)}, u32[]{:S(2)}, u32[]{:S(2)}) collective-permute-start(f32[3,64,1]{2,1,0:T(8,128)S(1)} %slice.525), channel_id=1, source_target_pairs={{0,1},{1,2},{2,3},{3,4},{4,5},{5,6},{6,7},{7,8},{8,9},{9,10},{10,1... | collective-permute-start | bytes 2312 | tf_op jit(solution)/shard_map/ppermute | solution.py:12
  350.6 1.9 collective-permute-start.3
  353.1 2.8 copy.65
  356.7 1.1 multiply_reduce_fusion.1
  357.8 104.9 %all-reduce.1 = (f32[]{:T(128)}, f32[]{:T(128)}) all-reduce(f32[]{:T(128)} %get-tuple-element.3, f32[]{:T(128)} %get-tuple-element.2), channel_id=1, replica_groups=mesh['gx'=32,'gy'=16] {'gx','gy'}, use_global_device_ids=true, to_apply=%region_2.3 | all-reduce | flops 2 | bytes 16 | tf_op jit(solution)/shard_map/psum | solution.py:62
  464.1 0.7 multiply_reduce_fusion
  464.8 95.7 %psum.44 = f32[]{:T(128)} all-reduce(f32[]{:T(128)} %get-tuple-element.6), channel_id=1, replica_groups=mesh['gx'=32,'gy'=16] {'gx','gy'}, use_global_device_ids=true, to_apply=%region_6.7 | all-reduce | flops 1 | bytes 8 | tf_op jit(solution)/shard_map/psum | solution.py:62
  562.3 2.7 collective-permute-start.4
  565.0 1.3 collective-permute-start.5
  566.4 4.1 collective-permute-start.6
  570.6 1.9 collective-permute-start.7
  572.6 3.9 collective-permute-done.7
  576.7 0.9 fusion.7
  577.9 99.6 %psum.45 = f32[]{:T(128)} all-reduce(f32[]{:T(128)} %fusion.7), channel_id=1, replica_groups=mesh['gx'=32,'gy'=16] {'gx','gy'}, use_global_device_ids=true, to_apply=%region_8.9 | all-reduce | flops 1 | bytes 8 | tf_op jit(solution)/shard_map/psum | solution.py:101
  678.9 2.6 copy.69
  681.5 7.7 gather_fusion
  689.2 1.8 fusion.2
  691.1 1.1 fusion.4
  692.3 152.7 %all-reduce.5.cloned.1.call-done = f32[512,192]{1,0:T(8,128)} async-done(((f32[512,192]{1,0:T(8,128)}), f32[512,192]{1,0:T(8,128)}) %all-reduce.5.cloned.1.call-update) | async-done | bytes 393232 | tf_op jit(solution)/shard_map/psum | solution.py:123
  845.7 119.4 %all-reduce.7.cloned.1.call-done = f32[512,192]{1,0:T(8,128)} async-done(((f32[512,192]{1,0:T(8,128)}), f32[512,192]{1,0:T(8,128)}) %all-reduce.7.cloned.1.call-update) | async-done | bytes 393232 | tf_op jit(solution)/shard_map/psum | solution.py:123
  965.1 1.3 constant_dynamic-slice_fusion
  (81 shorter events, 4.2 us)
Async XLA Ops:
  7.2 837.9 %all-reduce.5.cloned.1.call-start = ((), (), s32[]{:S(2)}) async-start(), calls=%async_computation | async-start | bytes 1048576 | tf_op jit(solution)/shard_map/psum | solution.py:123
  92.0 8.6 copy-start.5
  306.8 3.0 copy-start
  306.8 3.0 copy-start.2
  306.8 3.0 copy-start.1
  310.1 46.6 %collective-permute-start = (f32[3,1,128]{2,1,0:T(1,128)S(1)}, f32[3,1,128]{2,1,0:T(1,128)S(1)}, u32[]{:S(2)}, u32[]{:S(2)}) collective-permute-start(f32[3,1,128]{2,1,0:T(1,128)S(1)} %pad_maximum_fusion.21), channel_id=1, source_target_pairs={{0,16},{16,32},{32,48},{48,64},{64,80},{80,96},{96,112},{112,128},... | collective-permute-start | bytes 4616 | tf_op jit(solution)/shard_map/ppermute | solution.py:12
  312.1 40.5 %copy-start.4 = (s32[2048]{0:T(1024)S(1)}, s32[2048]{0:T(1024)}, u32[]{:S(2)}) copy-start(s32[2048]{0:T(1024)} %param.17) | copy-start | bytes 24580
  312.1 40.5 %copy-start.3 = (f32[3,2048]{1,0:T(4,128)S(1)}, f32[3,2048]{1,0:T(4,128)}, u32[]{:S(2)}) copy-start(f32[3,2048]{1,0:T(4,128)} %param.18) | copy-start | bytes 73732
  312.1 44.6 %collective-permute-start.1 = (f32[3,1,128]{2,1,0:T(1,128)S(1)}, f32[3,1,128]{2,1,0:T(1,128)S(1)}, u32[]{:S(2)}, u32[]{:S(2)}) collective-permute-start(f32[3,1,128]{2,1,0:T(1,128)S(1)} %pad_maximum_fusion.20), channel_id=1, source_target_pairs={{16,0},{32,16},{48,32},{64,48},{80,64},{96,80},{112,96},{128,112},... | collective-permute-start | bytes 4616 | tf_op jit(solution)/shard_map/ppermute | solution.py:12
  313.6 42.4 %collective-permute-start.2 = (f32[3,64,1]{2,1,0:T(8,128)S(1)}, f32[3,64,1]{2,1,0:T(8,128)S(1)}, u32[]{:S(2)}, u32[]{:S(2)}) collective-permute-start(f32[3,64,1]{2,1,0:T(8,128)S(1)} %slice.525), channel_id=1, source_target_pairs={{0,1},{1,2},{2,3},{3,4},{4,5},{5,6},{6,7},{7,8},{8,9},{9,10},{10,1... | collective-permute-start | bytes 2312 | tf_op jit(solution)/shard_map/ppermute | solution.py:12
  350.6 5.9 collective-permute-start.3
  562.3 14.4 %collective-permute-start.4 = (f32[3,1,128]{2,1,0:T(1,128)S(1)}, f32[3,1,128]{2,1,0:T(1,128)S(1)}, u32[]{:S(2)}, u32[]{:S(2)}) collective-permute-start(f32[3,1,128]{2,1,0:T(1,128)S(1)} %pad_maximum_fusion.19), channel_id=1, source_target_pairs={{0,16},{16,32},{32,48},{48,64},{64,80},{80,96},{96,112},{112,128},... | collective-permute-start | bytes 4616 | tf_op jit(solution)/shard_map/ppermute | solution.py:12
  565.0 11.7 %collective-permute-start.5 = (f32[3,1,128]{2,1,0:T(1,128)S(1)}, f32[3,1,128]{2,1,0:T(1,128)S(1)}, u32[]{:S(2)}, u32[]{:S(2)}) collective-permute-start(f32[3,1,128]{2,1,0:T(1,128)S(1)} %pad_maximum_fusion.18), channel_id=1, source_target_pairs={{16,0},{32,16},{48,32},{64,48},{80,64},{96,80},{112,96},{128,112},... | collective-permute-start | bytes 4616 | tf_op jit(solution)/shard_map/ppermute | solution.py:12
  566.4 6.1 collective-permute-start.6
  570.6 5.9 collective-permute-start.7
  681.5 9.6 copy-start.6
  692.3 272.8 %all-reduce.7.cloned.1.call-start = ((), (), s32[]{:S(2)}) async-start(), calls=%async_computation.1 | async-start | bytes 1048576 | tf_op jit(solution)/shard_map/psum | solution.py:123
Sparse Core Ops, SparseCore 0:
  692.4 152.5 all-reduce.4
  847.4 117.5 all-reduce.6
